TPU v7x, 256 devices: a whole 4x4x8 slice. The times are simulated.
256 devices in a mesh: head: 16 (over z, core), tail: 16 (over y, x).
Axes of the slice: x: 4, y: 4, z: 8, core: 2. Of those that a mesh axis runs over, the one named last changes fastest.
Arguments:
- head_emb: bfloat16 [131072, 800], P(('head', 'tail')), may hold values from -48 to 48
- head_state: float32 [131072], P(('head', 'tail')), may hold values from 0.01 to 1
- tail_emb: bfloat16 [64, 128, 800], P('tail'), may hold values from -1.5 to 1.5
- tail_state: float32 [64, 128], P('tail'), may hold values from 0.01 to 1
- relation_emb: bfloat16 [1024, 800], replicated, may hold values from -3.5 to 3.5
- head_rows: int32 [1024, 256], P(('head', 'tail')), may hold values from 0 to 511
- relations: int32 [1024, 256], P(('head', 'tail')), may hold values from 0 to 1023
- tail_offsets: int32 [1024, 256], P(('head', 'tail')), may hold values from 0 to 127
- tail_owner: int32 [1024, 1], P(('head', 'tail')), may hold values from 0 to 15; in each aligned block of 4 rows (0 to 3, 4 to 7, ...) at most 2 rows name the same one
- tail_local: int32 [1024], P(('head', 'tail')), may hold values from 0 to 3
- block_count: int32 [256], P(('head', 'tail')), may hold values from 1 to 4, as said below
- neg_blocks: int32 [8], replicated, may hold values from 0 to 63, as said below
Outputs:
- head_new: bfloat16 [131072, 800], P(('head', 'tail'))
- head_state_new: float32 [131072], P(('head', 'tail'))
- tail_new: bfloat16 [64, 128, 800], P('tail')
- tail_state_new: float32 [64, 128], P('tail')
Inputs may be any that keep to these rules, and one draw needn't show every extreme that they name: `tail_owner`: no tail index owns the tail blocks of more than 2 edge block slots of one device, and in some devices one owns exactly 2. `block_count`: some device has all 4 slots live. `neg_blocks`: distinct tail blocks; the last tail block is always among them.
All inputs are finite; a program needn't handle non-finite values.
Results may differ from a plain program's by a relative error of at most 0.0012.
The roundings to bfloat16 on the way count: a program that leaves them out, or rounds other values in their place, can miss the bound.
Values may be sent and summed in bfloat16 or wider, within the bound.
A program may use at most 128 MiB of HBM per device.

v0:
```python
import jax
import jax.numpy as jnp
from jax import lax
from jax.sharding import PartitionSpec as P

LEARN_RATE = 0.3


def complex_product(left, right):
    half_width = left.shape[-1] // 2
    left_re, left_im = (left[..., :half_width], left[..., half_width:])
    right_re, right_im = (right[..., :half_width], right[..., half_width:])
    return jnp.concatenate(
        [left_re * right_re - left_im * right_im, left_re * right_im + left_im * right_re], axis=-1
    )


def conj_product(left, right):
    half_width = left.shape[-1] // 2
    left_re, left_im = (left[..., :half_width], left[..., half_width:])
    right_re, right_im = (right[..., :half_width], right[..., half_width:])
    return jnp.concatenate(
        [left_re * right_re + left_im * right_im, left_im * right_re - left_re * right_im], axis=-1
    )


def row_adagrad(embedding, adagrad_state, gradient):
    state_next = adagrad_state + jnp.mean(gradient * gradient, axis=-1)
    updated = (
        embedding.astype(jnp.float32) - LEARN_RATE * gradient / jnp.sqrt(state_next)[..., None]
    )
    return (updated.astype(jnp.bfloat16), state_next)


def per_device(
    head_emb,
    head_state,
    tail_emb,
    tail_state,
    relation_emb,
    head_rows,
    relations,
    tail_offsets,
    tail_owner,
    tail_local,
    block_count,
    neg_blocks,
):
    block_total = tail_local.shape[0]
    edge_count = head_rows.shape[1]
    row_width = head_emb.shape[1]
    span_rows = tail_emb.shape[1]
    owned_blocks = tail_emb.shape[0]
    neg_count = neg_blocks.shape[0]
    peer_count = lax.axis_size("tail")
    head_count = lax.axis_size("head")
    tail_rank = lax.axis_index("tail")
    head_rank = lax.axis_index("head")
    piece = span_rows // head_count
    capacity = max(2, (2 * block_total + peer_count - 1) // peer_count)
    owner_rank = tail_owner[:, 0]
    positions = jnp.arange(block_total, dtype=jnp.int32)
    same_owner = owner_rank[:, None] == owner_rank[None, :]
    earlier = positions[None, :] < positions[:, None]
    slot_index = jnp.sum((same_owner & earlier).astype(jnp.int32), axis=1)
    slot_place = owner_rank * capacity + slot_index
    global_block = owner_rank * owned_blocks + tail_local
    slot_ids = (
        jnp.zeros((peer_count * capacity,), jnp.int32)
        .at[slot_place]
        .set(tail_local)
        .reshape(peer_count, capacity)
    )
    incoming_ids = lax.all_to_all(slot_ids, "tail", split_axis=0, concat_axis=0, tiled=True)
    my_rows = lax.dynamic_slice_in_dim(tail_emb, head_rank * piece, piece, axis=1)
    table = lax.all_gather(
        my_rows.reshape(owned_blocks * piece, row_width), ("head", "tail"), axis=0, tiled=True
    )

    def table_row(block, offset):
        return (
            (offset // piece * peer_count + block // owned_blocks) * owned_blocks
            + block % owned_blocks
        ) * piece + offset % piece

    neg_offset = (
        jnp.arange(head_count, dtype=jnp.int32)[:, None, None] * piece
        + jnp.arange(piece, dtype=jnp.int32)[None, None, :]
    )
    neg_index = table_row(neg_blocks[None, :, None], neg_offset).reshape(-1)
    mine_ids = neg_blocks - tail_rank * owned_blocks
    total_edges = block_total * edge_count
    flat_rows = head_rows.reshape(-1)
    block_of = jnp.arange(total_edges, dtype=jnp.int32) // edge_count
    live_rows = (block_of < block_count[0]).astype(jnp.float32)
    tail_index = block_of * span_rows + tail_offsets.reshape(-1)
    vector_index = table_row(global_block[:, None], tail_offsets).reshape(-1)
    relation_vectors = jnp.take(relation_emb, relations.reshape(-1), axis=0)
    head_vectors = jnp.take(head_emb, flat_rows, axis=0)
    query = complex_product(
        head_vectors.astype(jnp.float32), relation_vectors.astype(jnp.float32)
    ).astype(jnp.bfloat16)
    negatives = jnp.take(table, neg_index, axis=0)
    tail_rows = jnp.take(table, vector_index, axis=0)
    query_float = query.astype(jnp.float32)
    positive = jnp.sum(query_float * tail_rows.astype(jnp.float32), axis=1)
    negative = lax.dot_general(
        query, negatives, (((1,), (1,)), ((), ())), preferred_element_type=jnp.float32
    )
    largest = jnp.maximum(positive, jnp.max(negative, axis=1))
    pos_exp = jnp.exp(positive - largest)
    neg_exp = jnp.exp(negative - largest[:, None])
    denominator = pos_exp + jnp.sum(neg_exp, axis=1)
    pos_grad = (pos_exp / denominator - 1.0) * live_rows
    neg_grad = (neg_exp / denominator[:, None] * live_rows[:, None]).astype(jnp.bfloat16)
    tail_part = pos_grad[:, None] * query_float
    block_grad = (
        jnp.zeros((block_total * span_rows, row_width), jnp.float32)
        .at[tail_index]
        .add(tail_part)
        .astype(jnp.bfloat16)
    )
    outgoing = (
        jnp.zeros((peer_count * capacity, span_rows, row_width), jnp.bfloat16)
        .at[slot_place]
        .set(block_grad.reshape(block_total, span_rows, row_width))
    )
    incoming = lax.all_to_all(
        outgoing.reshape(peer_count, capacity, span_rows, row_width),
        "tail",
        split_axis=0,
        concat_axis=0,
        tiled=True,
    )
    neg_part = lax.dot_general(
        neg_grad, query, (((0,), (0,)), ((), ())), preferred_element_type=jnp.float32
    )
    neg_piece = lax.psum_scatter(neg_part, "head", scatter_dimension=0, tiled=True)
    neg_all = lax.psum(neg_piece, "tail").reshape(neg_count, piece, row_width)
    query_grad = pos_grad[:, None] * tail_rows.astype(jnp.float32) + jnp.dot(
        neg_grad, negatives, preferred_element_type=jnp.float32
    )
    head_grad = (
        jnp.zeros(head_emb.shape, jnp.float32)
        .at[flat_rows]
        .add(conj_product(query_grad, relation_vectors.astype(jnp.float32)))
    )
    head_updated, head_state_updated = row_adagrad(head_emb, head_state, head_grad)
    incoming, head_updated = lax.optimization_barrier((incoming, head_updated))
    arrived = incoming.reshape(peer_count * capacity, head_count, piece, row_width)
    arrived_ids = incoming_ids.reshape(-1)
    tail_grad = jnp.stack(
        [
            jnp.sum(
                jnp.where(
                    (arrived_ids == b)[:, None, None, None], arrived.astype(jnp.float32), 0.0
                ),
                axis=0,
            )
            for b in range(owned_blocks)
        ],
        axis=1,
    )
    tail_piece = lax.psum_scatter(
        tail_grad.reshape(head_count * owned_blocks * piece, row_width),
        "head",
        scatter_dimension=0,
        tiled=True,
    ).reshape(owned_blocks, piece, row_width)
    own_negs = jnp.stack(
        [
            jnp.sum(jnp.where((mine_ids == b)[:, None, None], neg_all, 0.0), axis=0)
            for b in range(owned_blocks)
        ],
        axis=0,
    )
    state_rows = lax.dynamic_slice_in_dim(tail_state, head_rank * piece, piece, axis=1)
    tail_updated, tail_state_updated = row_adagrad(my_rows, state_rows, tail_piece + own_negs)
    tail_updated = lax.all_gather(
        tail_updated.reshape(owned_blocks * piece, row_width), "head", axis=0, tiled=True
    )
    tail_updated = (
        tail_updated.reshape(head_count, owned_blocks, piece, row_width)
        .transpose(1, 0, 2, 3)
        .reshape(owned_blocks, span_rows, row_width)
    )
    tail_state_updated = (
        lax.all_gather(tail_state_updated, "head", axis=0, tiled=False)
        .transpose(1, 0, 2)
        .reshape(owned_blocks, span_rows)
    )
    return (head_updated, head_state_updated, tail_updated, tail_state_updated)


def solution(mesh):
    placed = (
        P(("head", "tail"), None),
        P(("head", "tail")),
        P("tail", None, None),
        P("tail", None),
        P(),
        P(("head", "tail"), None),
        P(("head", "tail"), None),
        P(("head", "tail"), None),
        P(("head", "tail"), None),
        P(("head", "tail")),
        P(("head", "tail")),
        P(),
    )
    return jax.shard_map(
        per_device,
        mesh=mesh,
        in_specs=placed,
        out_specs=(
            P(("head", "tail"), None),
            P(("head", "tail")),
            P("tail", None, None),
            P("tail", None),
        ),
        check_vma=False,
    )
```

profile of v0, /device:TPU:1, one launch (start us, length us, event | category | flops | bytes accessed | tf_op | source)
XLA Modules:
  0.0 508.9 jit_solution(6795767045325392924)
XLA Ops:
  7.3 1.0 copy-done
  8.3 0.3 constant_dynamic-slice_fusion
  8.6 0.9 copy.164
  9.6 0.2 convert_reduce_fusion
  9.8 0.6 scatter_custom_fusion.3
  10.3 0.7 all_to_all.10
  11.0 7.6 %all-to-all-start.1 = ((s32[16,1,2]{2,1,0:T(1,128)}), s32[16,1,2]{2,1,0:T(1,128)S(1)}, u32[]{:S(2)}, u32[]{:S(2)}) async-start(s32[16,1,2]{2,1,0:T(1,128)} %bitcast.10), calls=%async_computation.1 | async-start | bytes 16384 | tf_op jit(solution)/shard_map/all_to_all | solution.py:74
  19.8 0.6 copy.136
  20.5 4.0 gather_fusion
  24.5 2.5 copy.137
  27.0 3.0 copy.138
  30.0 5.3 %gather_fusion.1 = bf16[1024,800]{1,0:T(8,128)(2,1)} fusion(bf16[1024,800]{1,0:T(8,128)(2,1)S(1)} %copy.138, s32[1024]{0:T(1024)S(1)} %broadcast_clamp_fusion), kind=kCustom, calls=%fused_computation.3 | custom fusion | bytes 3280896 | tf_op jit(solution)/shard_map/jit(_take)/gather | solution.py:98
  35.3 3.9 copy.139
  39.3 0.2 select_convert_fusion.1
  39.5 1.2 copy-done.6
  40.7 0.2 select_convert_fusion
  40.9 1.7 copy-done.2
  42.6 0.9 subtract_convert_fusion.1
  43.5 95.8 %all-gather.4.cloned.1.call-done = bf16[8192,800]{1,0:T(8,128)(2,1)} async-done(((bf16[32,800]{1,0:T(8,128)(2,1)}), bf16[8192,800]{1,0:T(8,128)(2,1)}) %all-gather.4.cloned.1.call-update) | async-done | bytes 13107216 | tf_op jit(solution)/shard_map/all_gather | solution.py:76
  139.3 12.8 %gather_fusion.2 = bf16[1024,800]{1,0:T(8,128)(2,1)} fusion(bf16[8192,800]{1,0:T(8,128)(2,1)} %all-gather.4.cloned.1.call-done, s32[1024]{0:T(1024)S(1)} %fusion.40), kind=kCustom, calls=%fused_computation.clone | custom fusion | bytes 3280896 | tf_op jit(solution)/shard_map/jit(_take)/gather | solution.py:104
  152.1 3.8 copy.141
  155.9 2.1 fusion.5
  158.0 12.8 %gather_fusion.3 = bf16[1024,800]{1,0:T(8,128)(2,1)} fusion(bf16[8192,800]{1,0:T(8,128)(2,1)} %all-gather.4.cloned.1.call-done, s32[1024]{0:T(1024)S(1)} %fusion.41), kind=kCustom, calls=%fused_computation.1.clone | custom fusion | bytes 3280896 | tf_op jit(solution)/shard_map/jit(_take)/gather | solution.py:103
  170.8 3.9 fusion.54
  174.8 0.6 fusion.4
  175.4 0.8 multiply_convert_fusion
  176.2 1.3 copy-done.8
  177.5 4.2 fusion.52
  181.7 2.2 convert_multiply_fusion.2
  183.9 4.9 copy.142
  188.8 10.7 %scatter_custom_fusion = f32[512,800]{1,0:T(8,128)S(1)} fusion(s32[1024]{0:T(1024)S(1)} %bitcast.128, f32[1024,800]{1,0:T(8,128)} %copy.142, f32[]{:T(128)} %constant.175.clone.1), kind=kCustom, calls=%fused_computation.40 | custom fusion | flops 819200 | bytes 1638912 | tf_op jit(solution)/shard_map/scatter-add | solution.py:120
  199.5 1.0 convert_element_type.58
  200.5 1.5 copy.143
  202.1 3.5 broadcast_in_dim.115
  205.6 2.7 scatter_fusion
  208.4 5.2 %all-to-all-start = ((bf16[16,2,128,800]{2,3,1,0:T(8,128)(2,1)}), bf16[16,2,128,800]{2,3,1,0:T(8,128)(2,1)}, u32[]{:S(2)}, u32[]{:S(2)}) async-start(bf16[16,2,128,800]{2,3,1,0:T(8,128)(2,1)} %bitcast.93), calls=%async_computation | async-start | bytes 13107200 | tf_op jit(solution)/shard_map/all_to_all | solution.py:128
  213.6 0.3 all-reduce.2.cloned.1.call-start
  214.3 4.5 fusion.6
  218.9 1.1 multiply_add_fusion
  220.0 2.0 pad_maximum_fusion
  221.9 4.9 copy.145
  226.8 10.7 %scatter_custom_fusion.2 = f32[512,800]{1,0:T(8,128)S(1)} fusion(s32[1024]{0:T(1024)S(1)} %bitcast.123, f32[1024,800]{1,0:T(8,128)} %copy.145, f32[]{:T(128)} %constant.175.clone.1), kind=kCustom, calls=%fused_computation.38 | custom fusion | flops 819200 | bytes 1638912 | tf_op jit(solution)/shard_map/scatter-add | solution.py:146
  237.5 0.2 multiply_reduce_fusion
  237.7 0.6 fusion.53
  238.3 1.4 subtract_convert_fusion
  239.6 71.6 %all-to-all-done = bf16[16,2,128,800]{2,3,1,0:T(8,128)(2,1)} async-done(((bf16[16,2,128,800]{2,3,1,0:T(8,128)(2,1)}), bf16[16,2,128,800]{2,3,1,0:T(8,128)(2,1)}, u32[]{:S(2)}, u32[]{:S(2)}) %all-to-all-start) | async-done | bytes 6553632 | tf_op jit(solution)/shard_map/all_to_all | solution.py:128
  311.3 7.9 %fusion = (f32[128,800]{0,1:T(8,128)S(1)}, f32[128,800]{0,1:T(8,128)S(1)}, f32[128,800]{0,1:T(8,128)S(1)}, f32[128,800]{0,1:T(8,128)S(1)}) fusion(bf16[16,2,128,800]{2,3,1,0:T(8,128)(2,1)} %all-to-all-done, pred[16,2]{1,0:T(8,128)(4,1)S(1)} %copy.148, pred[16,2]{1,0:T(8,128)(4,1)S(1)} %copy.151, pred[16,2]{1,0:T(8,128)(4,1)S(1)} %copy.154, ...), kind=kLoop, calls=%fused_computation.12 | loop fusion | flops 29081600 | bytes 8192128 | tf_op jit(solution)/shard_map/reduce_sum | solution.py:154
  319.2 0.2 copy.149
  319.4 0.2 copy.152
  319.6 0.2 copy.155
  319.8 0.2 copy.158
  320.0 0.1 pad_maximum_fusion.1
  320.1 1.5 copy.159
  321.7 1.1 copy-done.7
  322.8 1.2 copy.162
  324.0 77.9 %all-reduce.2.cloned.1.call-done = f32[8,8,800]{2,1,0:T(8,128)} async-done(((f32[8,8,800]{2,1,0:T(8,128)}), f32[8,8,800]{2,1,0:T(8,128)}) %all-reduce.2.cloned.1.call-update) | async-done | bytes 204816 | tf_op jit(solution)/shard_map/psum | solution.py:139
  401.9 1.1 select_reduce_fusion.3
  403.0 58.7 %reduce-scatter.3.cloned.1.call-done = f32[32,800]{1,0:T(8,128)} async-done(((f32[512,800]{1,0:T(8,128)}), f32[32,800]{1,0:T(8,128)}) %reduce-scatter.3.cloned.1.call-update) | async-done | bytes 102416 | tf_op jit(solution)/shard_map/reduce_scatter | solution.py:164
  461.8 1.0 fusion.13
  463.0 17.6 %all-gather.1 = f32[16,4,8]{2,1,0:T(4,128)S(1)} all-gather(f32[1,4,8]{2,1,0:T(4,128)S(1)} %get-tuple-element.49), channel_id=2, replica_groups=mesh['head'=16,'tail'=16] {'head'}, dimensions={0}, use_global_device_ids=true | all-gather | bytes 2176 | tf_op jit(solution)/shard_map/all_gather | solution.py:188
  480.6 0.7 reshape.451
  481.2 1.0 fusion.18
  482.2 18.8 %all_gather.13 = bf16[512,800]{1,0:T(8,128)(2,1)S(1)} all-gather(bf16[32,800]{1,0:T(8,128)(2,1)S(1)} %fusion.18), channel_id=1, replica_groups=mesh['head'=16,'tail'=16] {'head'}, dimensions={0}, use_global_device_ids=true | all-gather | bytes 870400 | tf_op jit(solution)/shard_map/all_gather | solution.py:179
  501.1 1.3 copy.163
  (83 shorter events, 1.5 us)
Async XLA Ops:
  7.2 1.2 copy-start
  7.2 2.4 copy-start.17
  7.2 2.6 copy-start.16
  7.2 12.1 %copy-start.11 = (s32[4,256]{1,0:T(4,128)S(1)}, s32[4,256]{1,0:T(4,128)}, u32[]{:S(2)}) copy-start(s32[4,256]{1,0:T(4,128)} %param.21) | copy-start | bytes 12292
  7.2 12.2 %copy-start.12 = (s32[4,256]{1,0:T(4,128)S(1)}, s32[4,256]{1,0:T(4,128)}, u32[]{:S(2)}) copy-start(s32[4,256]{1,0:T(4,128)} %param.20) | copy-start | bytes 12292
  7.2 12.3 %copy-start.13 = (s32[4,256]{1,0:T(4,128)S(1)}, s32[4,256]{1,0:T(4,128)}, u32[]{:S(2)}) copy-start(s32[4,256]{1,0:T(4,128)} %param.19) | copy-start | bytes 12292
  7.2 12.3 %copy-start.18 = (s32[8]{0:T(128)S(1)}, s32[8]{0:T(128)}, u32[]{:S(2)}) copy-start(s32[8]{0:T(128)} %param.25) | copy-start | bytes 100
  7.2 12.6 %copy-start.9 = (bf16[512,800]{0,1:T(8,128)(2,1)S(1)}, bf16[512,800]{0,1:T(8,128)(2,1)}, u32[]{:S(2)}) copy-start(bf16[512,800]{0,1:T(8,128)(2,1)} %param.14) | copy-start | bytes 2457604
  7.3 132.1 %all-gather.4.cloned.1.call-start = ((), (), s32[]{:S(2)}) async-start(), calls=%async_computation.4 | async-start | bytes 14737408 | tf_op jit(solution)/shard_map/all_gather | solution.py:76
  11.0 197.3 %all-to-all-start.1 = ((s32[16,1,2]{2,1,0:T(1,128)}), s32[16,1,2]{2,1,0:T(1,128)S(1)}, u32[]{:S(2)}, u32[]{:S(2)}) async-start(s32[16,1,2]{2,1,0:T(1,128)} %bitcast.10), calls=%async_computation.1 | async-start | bytes 16384 | tf_op jit(solution)/shard_map/all_to_all | solution.py:74
  18.6 292.6 %reduce-scatter.5.cloned.1.call-start = ((), (), s32[]{:S(2)}) async-start(), calls=%async_computation.6 | async-start | bytes 3899392 | tf_op jit(solution)/shard_map/reduce_scatter | solution.py:138
  35.3 4.0 copy-start.5
  39.3 1.4 copy-start.6
  40.9 1.7 copy-start.2
  176.2 1.4 copy-start.8
  208.4 5.9 %copy-start.4 = (bf16[1024,800]{0,1:T(8,128)(2,1)S(1)}, bf16[1024,800]{0,1:T(8,128)(2,1)}, u32[]{:S(2)}) copy-start(bf16[1024,800]{0,1:T(8,128)(2,1)} %copy.141) | copy-start | bytes 4915204
  208.4 102.8 %all-to-all-start = ((bf16[16,2,128,800]{2,3,1,0:T(8,128)(2,1)}), bf16[16,2,128,800]{2,3,1,0:T(8,128)(2,1)}, u32[]{:S(2)}, u32[]{:S(2)}) async-start(bf16[16,2,128,800]{2,3,1,0:T(8,128)(2,1)} %bitcast.93), calls=%async_computation | async-start | bytes 13107200 | tf_op jit(solution)/shard_map/all_to_all | solution.py:128
  213.6 188.4 %all-reduce.2.cloned.1.call-start = ((), (), s32[]{:S(2)}) async-start(), calls=%async_computation.7 | async-start | bytes 458752 | tf_op jit(solution)/shard_map/psum | solution.py:139
  214.3 4.5 copy-start.3
  226.8 10.9 %copy-start.15 = (f32[512]{0:T(512)S(1)}, f32[512]{0:T(512)}, u32[]{:S(2)}) copy-start(f32[512]{0:T(512)} %param.15) | copy-start | bytes 6148
  311.3 150.5 %reduce-scatter.3.cloned.1.call-start = ((), (), s32[]{:S(2)}) async-start(), calls=%async_computation.5 | async-start | bytes 1949696 | tf_op jit(solution)/shard_map/reduce_scatter | solution.py:164
  321.6 1.2 copy-start.7
  321.6 141.3 %copy-start.14 = (f32[4,128]{1,0:T(4,128)S(1)}, f32[4,128]{1,0:T(4,128)}, u32[]{:S(2)}) copy-start(f32[4,128]{1,0:T(4,128)} %param.17) | copy-start | bytes 6148
  321.6 159.6 %copy-start.10 = (bf16[4,8,800]{2,1,0:T(8,128)(2,1)S(1)}, bf16[4,8,800]{2,1,0:T(8,128)(2,1)}, u32[]{:S(2)}) copy-start(bf16[4,8,800]{2,1,0:T(8,128)(2,1)} %copy.164) | copy-start | bytes 153604
  482.2 20.1 %copy-start.1 = (bf16[4,128,800]{1,2,0:T(8,128)(2,1)S(1)}, bf16[4,128,800]{1,2,0:T(8,128)(2,1)}, u32[]{:S(2)}) copy-start(bf16[4,128,800]{1,2,0:T(8,128)(2,1)} %param.16) | copy-start | bytes 2457604
Sparse Core Ops, SparseCore 0:
  12.2 127.0 all-gather.3
  181.8 57.1 reduce-scatter.4
  311.4 90.5 all-reduce.1
  404.3 57.3 reduce-scatter.2
where the time goes:
time: 510 us; the launch traced here: 509 us
  waiting for transfers between devices  304 us (60%)
  local copies, waits for them, and re-layouts  81.4 us (16%)
  other arithmetic  46.3 us (9%)
  blocking collectives  36.4 us (7%)
  between operations  14.9 us (3%)
  starting transfers between devices  13.1 us (3%)
  matrix products  12.6 us (2%)
    all_gather x1, waiting for transfers between devices, per_device(): lax.all_gather(my_rows.reshape(owned_blocks * piece, row_width), ('head',...  95.8 us
    psum x1, waiting for transfers between devices, per_device(): neg_all = lax.psum(neg_piece, 'tail').reshape(neg_count, piece, row_width)  77.9 us
    all_to_all x1, waiting for transfers between devices, per_device(): lax.all_to_all(outgoing.reshape(peer_count, capacity, span_rows, row_widt...  71.6 us
    reduce_scatter x1, waiting for transfers between devices, per_device(): lax.psum_scatter(tail_grad.reshape(head_count * owned_blocks * piece, row...  58.7 us
    all_gather x1, blocking collectives, per_device(): lax.all_gather(tail_updated.reshape(owned_blocks * piece, row_width), 'he...  18.8 us
    all_gather x1, blocking collectives, per_device(): lax.all_gather(tail_state_updated, 'head', axis=0, tiled=False)  17.6 us
    gather x2, local copies, waits for them, and re-layouts, per_device(): tail_rows = jnp.take(table, vector_index, axis=0)  16.6 us
    unnamed x49, local copies, waits for them, and re-layouts  13.4 us
  transfers between devices with their start and end apart: 6, of which 4 were waited for; matrix products, arithmetic and copies ran while one was open for 25% of the time, Pallas kernels for 0%

commit v1 on v0

--- a/solution.py
+++ b/solution.py
@@ -1,9 +1,17 @@
+import functools
 import jax
 import jax.numpy as jnp
 from jax import lax
 from jax.sharding import PartitionSpec as P
 
 LEARN_RATE = 0.3
+
+
+def cover_region(row_data, group_axis):
+    return lax.all_gather(row_data, group_axis).sum(axis=0)
+
+
+link_slabs = functools.partial(cover_region, group_axis="tail")
 
 
 def complex_product(left, right):
@@ -136,7 +144,7 @@
         neg_grad, query, (((0,), (0,)), ((), ())), preferred_element_type=jnp.float32
     )
     neg_piece = lax.psum_scatter(neg_part, "head", scatter_dimension=0, tiled=True)
-    neg_all = lax.psum(neg_piece, "tail").reshape(neg_count, piece, row_width)
+    neg_all = link_slabs(neg_piece).reshape(neg_count, piece, row_width)
     query_grad = pos_grad[:, None] * tail_rows.astype(jnp.float32) + jnp.dot(
         neg_grad, negatives, preferred_element_type=jnp.float32
     )

time: 510 us -> 452 us (0.89)
  waiting for transfers between devices: 304 us -> 246 us
    psum x1 -> x0, waiting for transfers between devices: 77.9 us -> none  [per_device(): neg_all = lax.psum(neg_piece, 'tail').reshape(neg_count, piece, row_width)]
    reduce_scatter x1, waiting for transfers between devices: 0.01 us -> 17 us  [per_device(): lax.psum_scatter(neg_part, 'head', scatter_dimension=0, tiled=True)]
    all_to_all x1, waiting for transfers between devices: 71.6 us -> 55.2 us  [per_device(): lax.all_to_all(outgoing.reshape(peer_count, capacity, span_rows, row_widt...]
    all_gather x0 -> x1, waiting for transfers between devices: none -> 12.7 us  [cover_region(): return lax.all_gather(row_data, group_axis).sum(axis=0)]
    all_gather x1, waiting for transfers between devices: 95.8 us -> 105 us  [per_device(): lax.all_gather(my_rows.reshape(owned_blocks * piece, row_width), ('head',...]
  transfers between devices with their start and end apart: 6 -> 6, of which waited for: 4 -> 5; matrix products, arithmetic and copies ran while one was open for 25% -> 20% of each run, Pallas kernels for 0% -> 0%
where the time goes in v1:
time: 452 us; the launch traced here: 451 us
  waiting for transfers between devices  246 us (54%)
  local copies, waits for them, and re-layouts  81.4 us (18%)
  other arithmetic  47.6 us (11%)
  blocking collectives  36.4 us (8%)
  between operations  14.9 us (3%)
  matrix products  12.6 us (3%)
  starting transfers between devices  12.2 us (3%)
    all_gather x1, waiting for transfers between devices, per_device(): lax.all_gather(my_rows.reshape(owned_blocks * piece, row_width), ('head',...  105 us
    reduce_scatter x1, waiting for transfers between devices, per_device(): lax.psum_scatter(tail_grad.reshape(head_count * owned_blocks * piece, row...  56.1 us
    all_to_all x1, waiting for transfers between devices, per_device(): lax.all_to_all(outgoing.reshape(peer_count, capacity, span_rows, row_widt...  55.2 us
    all_gather x1, blocking collectives, per_device(): lax.all_gather(tail_updated.reshape(owned_blocks * piece, row_width), 'he...  18.8 us
    all_gather x1, blocking collectives, per_device(): lax.all_gather(tail_state_updated, 'head', axis=0, tiled=False)  17.6 us
    reduce_scatter x1, waiting for transfers between devices, per_device(): lax.psum_scatter(neg_part, 'head', scatter_dimension=0, tiled=True)  17 us
    gather x2, local copies, waits for them, and re-layouts, per_device(): tail_rows = jnp.take(table, vector_index, axis=0)  16.6 us
    unnamed x49, local copies, waits for them, and re-layouts  13.4 us
  transfers between devices with their start and end apart: 6, of which 5 were waited for; matrix products, arithmetic and copies ran while one was open for 20% of the time, Pallas kernels for 0%

profile of v1, /device:TPU:1, one launch (start us, length us, event | category | flops | bytes accessed | tf_op | source)
XLA Modules:
  0.0 451.0 jit_solution(15271585586016614107)
XLA Ops:
  7.3 1.0 copy-done
  8.3 0.3 constant_dynamic-slice_fusion
  8.6 0.9 copy.164
  10.8 0.6 copy.136
  11.4 4.0 gather_fusion
  15.4 2.5 copy.137
  17.9 3.0 copy.138
  21.0 5.3 %gather_fusion.1 = bf16[1024,800]{1,0:T(8,128)(2,1)} fusion(bf16[1024,800]{1,0:T(8,128)(2,1)S(1)} %copy.138, s32[1024]{0:T(1024)S(1)} %broadcast_clamp_fusion), kind=kCustom, calls=%fused_computation.3 | custom fusion | bytes 3280896 | tf_op jit(solution)/shard_map/jit(_take)/gather | solution.py:106
  26.2 3.9 copy.139
  30.2 0.2 select_convert_fusion.1
  30.4 1.2 copy-done.6
  31.6 0.2 select_convert_fusion
  31.9 1.7 copy-done.2
  33.5 0.9 subtract_convert_fusion.1
  34.4 104.9 %all-gather.6.cloned.1.call-done = bf16[8192,800]{1,0:T(8,128)(2,1)} async-done(((bf16[32,800]{1,0:T(8,128)(2,1)}), bf16[8192,800]{1,0:T(8,128)(2,1)}) %all-gather.6.cloned.1.call-update) | async-done | bytes 13107216 | tf_op jit(solution)/shard_map/all_gather | solution.py:84
  139.3 12.8 %gather_fusion.2 = bf16[1024,800]{1,0:T(8,128)(2,1)} fusion(bf16[8192,800]{1,0:T(8,128)(2,1)} %all-gather.6.cloned.1.call-done, s32[1024]{0:T(1024)S(1)} %fusion.44), kind=kCustom, calls=%fused_computation.clone | custom fusion | bytes 3280896 | tf_op jit(solution)/shard_map/jit(_take)/gather | solution.py:112
  152.2 3.8 copy.141
  155.9 2.1 fusion.5
  158.0 12.8 %gather_fusion.3 = bf16[1024,800]{1,0:T(8,128)(2,1)} fusion(bf16[8192,800]{1,0:T(8,128)(2,1)} %all-gather.6.cloned.1.call-done, s32[1024]{0:T(1024)S(1)} %fusion.45), kind=kCustom, calls=%fused_computation.1.clone | custom fusion | bytes 3280896 | tf_op jit(solution)/shard_map/jit(_take)/gather | solution.py:111
  170.8 3.9 fusion.58
  174.8 0.6 fusion.4
  175.4 0.8 multiply_convert_fusion
  176.2 1.3 copy-done.8
  177.5 4.2 fusion.56
  181.7 0.2 convert_reduce_fusion
  181.9 0.6 scatter_custom_fusion.3
  182.5 0.7 all_to_all.10
  183.2 5.0 %all-to-all-start.1 = ((s32[16,1,2]{2,1,0:T(1,128)}), s32[16,1,2]{2,1,0:T(1,128)S(1)}, u32[]{:S(2)}, u32[]{:S(2)}) async-start(s32[16,1,2]{2,1,0:T(1,128)} %bitcast.10), calls=%async_computation.1 | async-start | bytes 16384 | tf_op jit(solution)/shard_map/all_to_all | solution.py:82
  188.2 2.2 convert_multiply_fusion.2
  190.4 4.9 %copy.142 = f32[1024,800]{1,0:T(8,128)} copy(f32[1024,800]{0,1:T(8,128)} %convert_multiply_fusion.2) | data formatting | bytes 6553600 | tf_op jit(solution)/shard_map/mul | solution.py:124
  195.3 10.7 %scatter_custom_fusion = f32[512,800]{1,0:T(8,128)S(1)} fusion(s32[1024]{0:T(1024)S(1)} %bitcast.141, f32[1024,800]{1,0:T(8,128)} %copy.142, f32[]{:T(128)} %constant.175.clone.1), kind=kCustom, calls=%fused_computation.40 | custom fusion | flops 819200 | bytes 1638912 | tf_op jit(solution)/shard_map/scatter-add | solution.py:128
  206.0 1.0 convert_element_type.58
  207.0 1.5 copy.143
  208.5 3.5 broadcast_in_dim.115
  212.1 2.7 scatter_fusion
  214.8 6.9 %all-to-all-start = ((bf16[16,2,128,800]{2,3,1,0:T(8,128)(2,1)}), bf16[16,2,128,800]{2,3,1,0:T(8,128)(2,1)}, u32[]{:S(2)}, u32[]{:S(2)}) async-start(bf16[16,2,128,800]{2,3,1,0:T(8,128)(2,1)} %bitcast.106), calls=%async_computation | async-start | bytes 13107200 | tf_op jit(solution)/shard_map/all_to_all | solution.py:136
  221.8 17.0 %reduce-scatter.5.cloned.1.call-done = f32[64,800]{1,0:T(8,128)} async-done(((f32[1024,800]{1,0:T(8,128)}), f32[64,800]{1,0:T(8,128)}) %reduce-scatter.5.cloned.1.call-update) | async-done | bytes 204816 | tf_op jit(solution)/shard_map/reduce_scatter | solution.py:146
  238.7 0.3 reduce-scatter.3.cloned.1.call-start
  239.5 4.5 %fusion.6 = f32[1024,800]{0,1:T(8,128)S(1)} fusion(bf16[1024,1024]{0,1:T(8,128)(2,1)} %copy-done.8, f32[1024]{0:T(1024)S(1)} %get-tuple-element.48, bf16[1024,800]{0,1:T(8,128)(2,1)S(1)} %copy-done.4, pred[1024]{0:T(1024)(128)(4,1)S(1)} %get-tuple-element.65, bf16[1024,800]{1,0:T(8,128)(2,1)} %gather_fusion.3, pred[1024]{0:T(1024)(128)(4,1)S(1)} %get-tuple-element.64), kind=kOutput, calls=%fused_computation.23 | convolution fusion | flops 1681817600 | bytes 8656896 | tf_op jit(solution)/shard_map/dot_general | solution.py:148
  244.0 1.1 multiply_add_fusion
  245.1 2.0 pad_maximum_fusion
  247.1 4.9 %copy.145 = f32[1024,800]{1,0:T(8,128)} copy(f32[1024,800]{0,1:T(8,128)} %pad_maximum_fusion) | data formatting | bytes 6553600 | tf_op jit(solution)/shard_map/concatenate | solution.py:30
  252.0 10.7 %scatter_custom_fusion.2 = f32[512,800]{1,0:T(8,128)S(1)} fusion(s32[1024]{0:T(1024)S(1)} %bitcast.136, f32[1024,800]{1,0:T(8,128)} %copy.145, f32[]{:T(128)} %constant.175.clone.1), kind=kCustom, calls=%fused_computation.38 | custom fusion | flops 819200 | bytes 1638912 | tf_op jit(solution)/shard_map/scatter-add | solution.py:154
  262.6 0.2 multiply_reduce_fusion
  262.8 0.6 fusion.57
  263.4 1.4 subtract_convert_fusion
  264.8 55.2 %all-to-all-done = bf16[16,2,128,800]{2,3,1,0:T(8,128)(2,1)} async-done(((bf16[16,2,128,800]{2,3,1,0:T(8,128)(2,1)}), bf16[16,2,128,800]{2,3,1,0:T(8,128)(2,1)}, u32[]{:S(2)}, u32[]{:S(2)}) %all-to-all-start) | async-done | bytes 6553632 | tf_op jit(solution)/shard_map/all_to_all | solution.py:136
  320.0 7.9 %fusion = (f32[128,800]{0,1:T(8,128)S(1)}, f32[128,800]{0,1:T(8,128)S(1)}, f32[128,800]{0,1:T(8,128)S(1)}, f32[128,800]{0,1:T(8,128)S(1)}) fusion(bf16[16,2,128,800]{2,3,1,0:T(8,128)(2,1)} %all-to-all-done, pred[16,2]{1,0:T(8,128)(4,1)S(1)} %copy.148, pred[16,2]{1,0:T(8,128)(4,1)S(1)} %copy.151, pred[16,2]{1,0:T(8,128)(4,1)S(1)} %copy.154, ...), kind=kLoop, calls=%fused_computation.12 | loop fusion | flops 29081600 | bytes 8192128 | tf_op jit(solution)/shard_map/reduce_sum | solution.py:162
  327.9 0.2 copy.149
  328.1 0.2 copy.152
  328.3 0.2 copy.155
  328.5 0.2 copy.158
  328.8 1.5 copy.159
  330.3 1.1 copy-done.7
  331.5 1.2 copy.162
  332.7 12.7 %all-gather.8.cloned.1.call-done = f32[1024,800]{1,0:T(8,128)} async-done(((f32[64,800]{1,0:T(8,128)}), f32[1024,800]{1,0:T(8,128)}) %all-gather.8.cloned.1.call-update) | async-done | bytes 3276816 | tf_op jit(solution)/shard_map/all_gather | solution.py:11
  345.4 2.3 reduce_sum.137
  347.8 56.1 %reduce-scatter.3.cloned.1.call-done = f32[32,800]{1,0:T(8,128)} async-done(((f32[512,800]{1,0:T(8,128)}), f32[32,800]{1,0:T(8,128)}) %reduce-scatter.3.cloned.1.call-update) | async-done | bytes 102416 | tf_op jit(solution)/shard_map/reduce_scatter | solution.py:172
  403.8 1.0 fusion.17
  405.0 17.6 %all-gather.2 = f32[16,4,8]{2,1,0:T(4,128)S(1)} all-gather(f32[1,4,8]{2,1,0:T(4,128)S(1)} %get-tuple-element.49), channel_id=3, replica_groups=mesh['head'=16,'tail'=16] {'head'}, dimensions={0}, use_global_device_ids=true | all-gather | bytes 2176 | tf_op jit(solution)/shard_map/all_gather | solution.py:196
  422.6 0.7 reshape.451
  423.3 1.0 fusion.22
  424.3 18.8 %all_gather.21 = bf16[512,800]{1,0:T(8,128)(2,1)S(1)} all-gather(bf16[32,800]{1,0:T(8,128)(2,1)S(1)} %fusion.22), channel_id=1, replica_groups=mesh['head'=16,'tail'=16] {'head'}, dimensions={0}, use_global_device_ids=true | all-gather | bytes 870400 | tf_op jit(solution)/shard_map/all_gather | solution.py:187
  443.2 1.3 copy.163
  (84 shorter events, 1.8 us)
Async XLA Ops:
  7.2 1.2 copy-start
  7.2 3.1 copy-start.16
  7.2 3.1 copy-start.17
  7.2 3.1 copy-start.13
  7.2 3.2 copy-start.11
  7.2 3.2 copy-start.12
  7.2 3.2 copy-start.18
  7.2 3.5 copy-start.9
  7.3 132.1 %all-gather.6.cloned.1.call-start = ((), (), s32[]{:S(2)}) async-start(), calls=%async_computation.4 | async-start | bytes 14737408 | tf_op jit(solution)/shard_map/all_gather | solution.py:84
  9.5 229.2 %reduce-scatter.5.cloned.1.call-start = ((), (), s32[]{:S(2)}) async-start(), calls=%async_computation.6 | async-start | bytes 3899392 | tf_op jit(solution)/shard_map/reduce_scatter | solution.py:146
  26.2 4.0 copy-start.5
  30.2 1.4 copy-start.6
  31.9 1.7 copy-start.2
  176.2 1.4 copy-start.8
  183.2 31.6 %all-to-all-start.1 = ((s32[16,1,2]{2,1,0:T(1,128)}), s32[16,1,2]{2,1,0:T(1,128)S(1)}, u32[]{:S(2)}, u32[]{:S(2)}) async-start(s32[16,1,2]{2,1,0:T(1,128)} %bitcast.10), calls=%async_computation.1 | async-start | bytes 16384 | tf_op jit(solution)/shard_map/all_to_all | solution.py:82
  214.8 24.7 %copy-start.4 = (bf16[1024,800]{0,1:T(8,128)(2,1)S(1)}, bf16[1024,800]{0,1:T(8,128)(2,1)}, u32[]{:S(2)}) copy-start(bf16[1024,800]{0,1:T(8,128)(2,1)} %copy.141) | copy-start | bytes 4915204
  214.8 105.2 %all-to-all-start = ((bf16[16,2,128,800]{2,3,1,0:T(8,128)(2,1)}), bf16[16,2,128,800]{2,3,1,0:T(8,128)(2,1)}, u32[]{:S(2)}, u32[]{:S(2)}) async-start(bf16[16,2,128,800]{2,3,1,0:T(8,128)(2,1)} %bitcast.106), calls=%async_computation | async-start | bytes 13107200 | tf_op jit(solution)/shard_map/all_to_all | solution.py:136
  221.7 123.7 %all-gather.8.cloned.1.call-start = ((), (), s32[]{:S(2)}) async-start(), calls=%async_computation.7 | async-start | bytes 3899392 | tf_op jit(solution)/shard_map/all_gather | solution.py:11
  238.7 165.1 %reduce-scatter.3.cloned.1.call-start = ((), (), s32[]{:S(2)}) async-start(), calls=%async_computation.5 | async-start | bytes 1949696 | tf_op jit(solution)/shard_map/reduce_scatter | solution.py:172
  239.5 4.5 %copy-start.3 = (f32[1024,800]{0,1:T(8,128)S(1)}, f32[1024,800]{0,1:T(8,128)}, u32[]{:S(2)}) copy-start(f32[1024,800]{0,1:T(8,128)} %copy-done.2) | copy-start | bytes 9830404
  252.0 10.9 %copy-start.15 = (f32[512]{0:T(512)S(1)}, f32[512]{0:T(512)}, u32[]{:S(2)}) copy-start(f32[512]{0:T(512)} %param.15) | copy-start | bytes 6148
  330.3 1.2 copy-start.7
  345.4 59.6 %copy-start.14 = (f32[4,128]{1,0:T(4,128)S(1)}, f32[4,128]{1,0:T(4,128)}, u32[]{:S(2)}) copy-start(f32[4,128]{1,0:T(4,128)} %param.17) | copy-start | bytes 6148
  345.4 78.0 %copy-start.10 = (bf16[4,8,800]{2,1,0:T(8,128)(2,1)S(1)}, bf16[4,8,800]{2,1,0:T(8,128)(2,1)}, u32[]{:S(2)}) copy-start(bf16[4,8,800]{2,1,0:T(8,128)(2,1)} %copy.164) | copy-start | bytes 153604
  424.3 20.1 %copy-start.1 = (bf16[4,128,800]{1,2,0:T(8,128)(2,1)S(1)}, bf16[4,128,800]{1,2,0:T(8,128)(2,1)}, u32[]{:S(2)}) copy-start(bf16[4,128,800]{1,2,0:T(8,128)(2,1)} %param.16) | copy-start | bytes 2457604
Sparse Core Ops, SparseCore 0:
  12.2 127.0 all-gather.5
  181.8 56.8 reduce-scatter.4
  241.1 104.1 all-gather.7
  347.8 56.0 reduce-scatter.2
